TPU v7x, 32 devices: a whole 2x2x4 slice. The times are simulated.
32 devices in a mesh: wide: 16 (over z, y, x), narrow: 2 (over core).
Axes of the slice: x: 2, y: 2, z: 4, core: 2. Of those that a mesh axis runs over, the one named last changes fastest.
Arguments:
- tokens: bfloat16 [16384, 1024], P(('wide', 'narrow')), may hold values from -6 to 6
- cotangent: bfloat16 [16384, 1024], P(('wide', 'narrow'))
- pages: int32 [16384], P('wide'), may hold values from 0 to 3, as said below
- boxes: int32 [2, 16384], P(None, 'wide'), may hold values from 0 to 1000, as said below
- gain_attn: bfloat16 [1024], replicated, may hold values from 0.099609375 to 1.8984375
- gain_ffn: bfloat16 [1024], replicated, may hold values from 0.099609375 to 1.8984375
- bias_tables: bfloat16 [96, 16], replicated, may hold values from -4 to 4
- w_query: bfloat16 [1024, 1024], P('wide', 'narrow'), may hold values from -0.046875 to 0.046875
- w_key: bfloat16 [1024, 1024], P('wide', 'narrow'), may hold values from -0.1875 to 0.1875
- w_value: bfloat16 [1024, 1024], P('wide', 'narrow'), may hold values from -0.1875 to 0.1875
- w_out: bfloat16 [1024, 1024], P('narrow', 'wide'), may hold values from -1 to 1
- w_gate: bfloat16 [1024, 2816], P('wide', 'narrow'), may hold values from -0.1875 to 0.1875
- w_up: bfloat16 [1024, 2816], P('wide', 'narrow'), may hold values from -0.1875 to 0.1875
- w_down: bfloat16 [2816, 1024], P('narrow', 'wide'), may hold values from -0.109375 to 0.109375
Outputs:
- output: bfloat16 [16384, 1024], P(('wide', 'narrow'))
- grad_tokens: float32 [16384, 1024], P(('wide', 'narrow'))
- grad_gain_attn: float32 [1024], replicated
- grad_gain_ffn: float32 [1024], replicated
- grad_bias_tables: float32 [96, 16], replicated
- grad_w_query: float32 [1024, 1024], P('wide', 'narrow')
- grad_w_key: float32 [1024, 1024], P('wide', 'narrow')
- grad_w_value: float32 [1024, 1024], P('wide', 'narrow')
- grad_w_out: float32 [1024, 1024], P('narrow', 'wide')
- grad_w_gate: float32 [1024, 2816], P('wide', 'narrow')
- grad_w_up: float32 [1024, 2816], P('wide', 'narrow')
- grad_w_down: float32 [2816, 1024], P('narrow', 'wide')
Inputs may be any that keep to these rules, and one draw needn't show every extreme that they name: Each aligned block of 1024 rows holds one page of up to 1024 rows or two pages of up to 512 rows each, the second starting at row 512 of the block; a value is the page's number within its block, 0 or 1, plus 2 on padding rows. A page has its patch rows first (784 of them for a page of the whole block, 196 otherwise), then text rows ending in an end token, then padding. Some block holds two pages. `boxes`: row 0 is the horizontal and row 1 the vertical centre of a row's box in thousandths of the page: patch rows carry the centre of their grid cell, text rows their word's box, end tokens 1000 and padding 0.
All inputs are finite; a program needn't handle non-finite values.
Results may differ from a plain program's by a relative error of at most 0.018.
Values may be sent and summed in bfloat16 or wider, within the bound.
A program may use at most 256 MiB of HBM per device.

v0:
```python
import jax
import jax.numpy as jnp
from jax import lax
from jax.sharding import PartitionSpec as P

HEADS = 16
HEAD_DIM = 64
BUCKETS = 32
PAGE = 512
epsilon = 1e-06
bucket_edges = (1, 2, 3, 4, 5, 6, 7, 8, 12, 16, 23, 32, 46, 64, 91)
layout_stretch = 4


def bucket_of(spacing, stretch_factor):
    magnitude = jnp.abs(spacing)
    counted = jnp.zeros(spacing.shape, jnp.int32)
    for border in bucket_edges:
        counted = counted + (magnitude >= border * stretch_factor).astype(jnp.int32)
    return counted + BUCKETS // 2 * (spacing > 0).astype(jnp.int32)


def norm_plain(values, gain_row):
    factor = lax.rsqrt(jnp.mean(values * values, axis=-1, keepdims=True) + epsilon)
    return values * factor * gain_row


def gated_unit(gate_pre, up_pre):
    return jax.nn.gelu(gate_pre, approximate=True) * up_pre


def times_transposed(left_side, right_side):
    return lax.dot_general(
        left_side, right_side, (((1,), (1,)), ((), ())), preferred_element_type=jnp.float32
    )


def transposed_times(left_side, right_side):
    return lax.dot_general(
        left_side, right_side, (((0,), (0,)), ((), ())), preferred_element_type=jnp.float32
    )


def layout_hots(row_start, key_start, row_count, key_count, boxes):
    row_ids = row_start + jnp.arange(row_count, dtype=jnp.int32)
    col_ids = key_start + jnp.arange(key_count, dtype=jnp.int32)
    linear_ids = bucket_of(col_ids[None, :] - row_ids[:, None], 1)
    box_query = lax.dynamic_slice_in_dim(boxes, row_start, row_count, 1)
    across = bucket_of(boxes[0][None, :] - box_query[0][:, None], layout_stretch)
    upward = bucket_of(boxes[1][None, :] - box_query[1][:, None], layout_stretch)
    labels = jnp.arange(BUCKETS, dtype=jnp.int32)[:, None, None]
    return jnp.concatenate(
        [linear_ids[None] == labels, across[None] == labels, upward[None] == labels], axis=0
    ).astype(jnp.bfloat16)


def block_bias(row_start, key_start, head_table_entries, boxes):
    sub_rows = min(128, PAGE)
    bias_parts = []
    for piece_id in range(PAGE // sub_rows):
        indicator_rows = layout_hots(
            row_start + piece_id * sub_rows, key_start, sub_rows, 2 * PAGE, boxes
        )
        bias_parts.append(
            jnp.einsum(
                "ai,anf->inf",
                head_table_entries,
                indicator_rows,
                preferred_element_type=jnp.float32,
            )
        )
    return jnp.concatenate(bias_parts, axis=1)


def block_table_grad(grad_scores, row_start, key_start, boxes, summed):
    sub_rows = min(128, PAGE)
    for piece_id in range(PAGE // sub_rows):
        indicator_rows = layout_hots(
            row_start + piece_id * sub_rows, key_start, sub_rows, 2 * PAGE, boxes
        )
        slice_portion = lax.slice_in_dim(
            grad_scores, piece_id * sub_rows, (piece_id + 1) * sub_rows, axis=1
        )
        summed = summed + jnp.einsum(
            "pru,dru->dp", slice_portion, indicator_rows, preferred_element_type=jnp.float32
        )
    return summed


def block_scores(block_id, query_all, key_all, head_table_entries, pages, boxes):
    row_start = block_id * PAGE
    key_start = block_id // 2 * (2 * PAGE)
    query_rows = lax.dynamic_slice_in_dim(query_all, row_start, PAGE, 0)
    scores = jnp.einsum("qhd,khd->hqk", query_rows, key_all, preferred_element_type=jnp.float32)
    scores = scores + block_bias(row_start, key_start, head_table_entries, boxes)
    page_rows = lax.dynamic_slice_in_dim(pages, row_start, PAGE, 0)
    allowed = pages[None, :] == page_rows[:, None] % 2
    return (jnp.where(allowed[None], scores, -1e30), row_start, key_start)


def local(
    tokens,
    cotangent,
    pages,
    boxes,
    gain_attn,
    gain_ffn,
    bias_tables,
    w_query,
    w_key,
    w_value,
    w_out,
    w_gate,
    w_up,
    w_down,
):
    narrow_size = lax.axis_size("narrow")
    heads_local = HEADS // narrow_size
    rows_local = tokens.shape[0]
    rows_wide = rows_local * narrow_size
    block_count = rows_wide // PAGE
    head_start = lax.axis_index("narrow") * heads_local
    head_table_entries = lax.dynamic_slice_in_dim(bias_tables, head_start, heads_local, 1)
    gathered = (
        lax.all_gather(w_query, "wide", axis=0, tiled=True),
        lax.all_gather(w_key, "wide", axis=0, tiled=True),
        lax.all_gather(w_value, "wide", axis=0, tiled=True),
        lax.all_gather(w_out, "wide", axis=1, tiled=True),
        lax.all_gather(w_gate, "wide", axis=0, tiled=True),
        lax.all_gather(w_up, "wide", axis=0, tiled=True),
        lax.all_gather(w_down, "wide", axis=1, tiled=True),
    )
    full_query, full_key, complete_value, full_out, full_gate, full_up, full_down = gathered
    tokens_float = tokens.astype(jnp.float32)
    gain_one = gain_attn.astype(jnp.float32)
    gain_two = gain_ffn.astype(jnp.float32)
    normed = lax.all_gather(
        norm_plain(tokens_float, gain_one).astype(jnp.bfloat16), "narrow", axis=0, tiled=True
    )
    query_all = (
        jnp.dot(normed, full_query, preferred_element_type=jnp.float32)
        .astype(jnp.bfloat16)
        .reshape(rows_wide, heads_local, HEAD_DIM)
    )
    key_all = (
        jnp.dot(normed, full_key, preferred_element_type=jnp.float32)
        .astype(jnp.bfloat16)
        .reshape(rows_wide, heads_local, HEAD_DIM)
    )
    value_all = (
        jnp.dot(normed, complete_value, preferred_element_type=jnp.float32)
        .astype(jnp.bfloat16)
        .reshape(rows_wide, heads_local, HEAD_DIM)
    )

    def forward_block(state_in, block_id):
        masked, row_start, key_start = block_scores(
            block_id, query_all, key_all, head_table_entries, pages, boxes
        )
        row_peak = jnp.max(masked, axis=-1, keepdims=True)
        powered = jnp.exp(masked - row_peak)
        row_total = jnp.sum(powered, axis=-1, keepdims=True)
        weights_low = (powered / row_total).astype(jnp.bfloat16)
        block_out = jnp.einsum(
            "hqk,khd->qhd", weights_low, value_all, preferred_element_type=jnp.float32
        ).astype(jnp.bfloat16)
        return (state_in, (block_out, row_peak + jnp.log(row_total)))

    block_ids = jnp.arange(block_count, dtype=jnp.int32)
    _, (attended_blocks, log_totals) = lax.scan(forward_block, jnp.int32(0), block_ids)
    attended = attended_blocks.reshape(rows_wide, heads_local * HEAD_DIM)
    hidden = tokens_float + lax.psum_scatter(
        jnp.dot(
            lax.slice_in_dim(attended, 0, rows_local * lax.axis_size("narrow"), axis=0),
            full_out,
            preferred_element_type=jnp.float32,
        ).astype(jnp.bfloat16),
        "narrow",
        scatter_dimension=0,
        tiled=True,
    ).astype(jnp.float32)
    normed_two = lax.all_gather(
        norm_plain(hidden, gain_two).astype(jnp.bfloat16), "narrow", axis=0, tiled=True
    )
    gate_pre = jnp.dot(normed_two, full_gate, preferred_element_type=jnp.float32)
    up_pre = jnp.dot(normed_two, full_up, preferred_element_type=jnp.float32)
    hidden_ff = gated_unit(gate_pre, up_pre).astype(jnp.bfloat16)
    output = (
        hidden
        + lax.psum_scatter(
            jnp.dot(
                lax.slice_in_dim(hidden_ff, 0, rows_local * lax.axis_size("narrow"), axis=0),
                full_down,
                preferred_element_type=jnp.float32,
            ).astype(jnp.bfloat16),
            "narrow",
            scatter_dimension=0,
            tiled=True,
        ).astype(jnp.float32)
    ).astype(jnp.bfloat16)
    gathered = (
        lax.all_gather(w_query, "wide", axis=0, tiled=True),
        lax.all_gather(w_key, "wide", axis=0, tiled=True),
        lax.all_gather(w_value, "wide", axis=0, tiled=True),
        lax.all_gather(w_out, "wide", axis=1, tiled=True),
        lax.all_gather(w_gate, "wide", axis=0, tiled=True),
        lax.all_gather(w_up, "wide", axis=0, tiled=True),
        lax.all_gather(w_down, "wide", axis=1, tiled=True),
    )
    full_query, full_key, complete_value, full_out, full_gate, full_up, full_down = gathered
    grad_output = lax.all_gather(cotangent, "narrow", axis=0, tiled=True)
    grad_w_down = transposed_times(hidden_ff, grad_output)
    grad_ff = times_transposed(grad_output, full_down)
    _, gated_pull = jax.vjp(gated_unit, gate_pre, up_pre)
    grad_gate, grad_up = gated_pull(grad_ff)
    grad_gate = grad_gate.astype(jnp.bfloat16)
    grad_up = grad_up.astype(jnp.bfloat16)
    grad_w_gate = transposed_times(normed_two, grad_gate)
    grad_w_up = transposed_times(normed_two, grad_up)
    gate_rows = lax.slice_in_dim(grad_gate, 0, rows_local * lax.axis_size("narrow"), axis=0)
    up_rows = lax.slice_in_dim(grad_up, 0, rows_local * lax.axis_size("narrow"), axis=0)
    grad_normed_two = lax.psum_scatter(
        (times_transposed(gate_rows, full_gate) + times_transposed(up_rows, full_up)).astype(
            jnp.bfloat16
        ),
        "narrow",
        scatter_dimension=0,
        tiled=True,
    ).astype(jnp.float32)
    _, norm_pull_two = jax.vjp(norm_plain, hidden, gain_two)
    grad_hidden_norm, grad_gain_two = norm_pull_two(grad_normed_two)
    grad_hidden = cotangent.astype(jnp.float32) + grad_hidden_norm
    grad_attn = lax.all_gather(grad_hidden.astype(jnp.bfloat16), "narrow", axis=0, tiled=True)
    grad_w_out = transposed_times(attended, grad_attn)
    grad_attended = (
        times_transposed(grad_attn, full_out)
        .astype(jnp.bfloat16)
        .reshape(block_count, PAGE, heads_local, HEAD_DIM)
    )

    def backward_block(state_in, inputs):
        key_grad, value_grad, table_grad = state_in
        block_id, grad_block, log_total = inputs
        masked, row_start, key_start = block_scores(
            block_id, query_all, key_all, head_table_entries, pages, boxes
        )
        probs = jnp.exp(masked - log_total)
        probs_low = probs.astype(jnp.bfloat16)
        query_rows = lax.dynamic_slice_in_dim(query_all, row_start, PAGE, 0)
        grad_probs = jnp.einsum(
            "qhd,khd->hqk", grad_block, value_all, preferred_element_type=jnp.float32
        )
        inner_row_index = jnp.sum(probs * grad_probs, axis=-1, keepdims=True)
        grad_scores = (probs * (grad_probs - inner_row_index)).astype(jnp.bfloat16)
        grad_query_block = jnp.einsum(
            "hqk,khd->qhd", grad_scores, key_all, preferred_element_type=jnp.float32
        ).astype(jnp.bfloat16)
        key_part = jnp.einsum(
            "hqk,qhd->khd", grad_scores, query_rows, preferred_element_type=jnp.float32
        )
        value_part = jnp.einsum(
            "hqk,qhd->khd", probs_low, grad_block, preferred_element_type=jnp.float32
        )
        key_grad = lax.dynamic_update_slice_in_dim(key_grad, key_grad + key_part, key_start, 0)
        value_grad = lax.dynamic_update_slice_in_dim(
            value_grad, value_grad + value_part, key_start, 0
        )
        table_grad = block_table_grad(grad_scores, row_start, key_start, boxes, table_grad)
        return ((key_grad, value_grad, table_grad), grad_query_block)

    empty_rows = jnp.zeros((rows_wide, heads_local, HEAD_DIM), jnp.float32)
    empty_table = jnp.zeros((3 * BUCKETS, heads_local), jnp.float32)
    (key_grad, value_grad, table_grad), query_blocks = lax.scan(
        backward_block,
        (empty_rows, empty_rows, empty_table),
        (block_ids, grad_attended, log_totals),
    )
    grad_queries = query_blocks.reshape(rows_wide, heads_local * HEAD_DIM)
    grad_keys = key_grad.astype(jnp.bfloat16).reshape(rows_wide, heads_local * HEAD_DIM)
    grad_values = value_grad.astype(jnp.bfloat16).reshape(rows_wide, heads_local * HEAD_DIM)
    grad_w_query = transposed_times(normed, grad_queries)
    grad_w_key = transposed_times(normed, grad_keys)
    grad_w_value = transposed_times(normed, grad_values)
    query_part = times_transposed(
        lax.slice_in_dim(grad_queries, 0, rows_local * lax.axis_size("narrow"), axis=0), full_query
    )
    key_side = times_transposed(grad_keys, full_key)
    value_side = times_transposed(grad_values, complete_value)
    grad_normed = lax.psum_scatter(
        (query_part + key_side + value_side).astype(jnp.bfloat16),
        "narrow",
        scatter_dimension=0,
        tiled=True,
    ).astype(jnp.float32)
    _, norm_pull_one = jax.vjp(norm_plain, tokens_float, gain_one)
    grad_tokens_norm, grad_gain_one = norm_pull_one(grad_normed)
    grad_tokens = grad_hidden + grad_tokens_norm
    table_full = lax.dynamic_update_slice(
        jnp.zeros((3 * BUCKETS, HEADS), jnp.float32), table_grad, (jnp.int32(0), head_start)
    )
    grad_gain_attn, grad_gain_ffn, grad_bias_tables = lax.psum(
        (grad_gain_one, grad_gain_two, table_full), ("wide", "narrow")
    )
    all_parts = (
        lax.psum_scatter(grad_w_query, "wide", scatter_dimension=0, tiled=True),
        lax.psum_scatter(grad_w_key, "wide", scatter_dimension=0, tiled=True),
        lax.psum_scatter(grad_w_value, "wide", scatter_dimension=0, tiled=True),
        lax.psum_scatter(grad_w_out, "wide", scatter_dimension=1, tiled=True),
        lax.psum_scatter(grad_w_gate, "wide", scatter_dimension=0, tiled=True),
        lax.psum_scatter(grad_w_up, "wide", scatter_dimension=0, tiled=True),
        lax.psum_scatter(grad_w_down, "wide", scatter_dimension=1, tiled=True),
    )
    shard_query, shard_key, shard_value, shard_out, shard_gate, shard_up, shard_down = all_parts
    return (
        output,
        grad_tokens,
        grad_gain_attn,
        grad_gain_ffn,
        grad_bias_tables,
        shard_query,
        shard_key,
        shard_value,
        shard_out,
        shard_gate,
        shard_up,
        shard_down,
    )


def solution(mesh):
    in_specs = (
        P(("wide", "narrow"), None),
        P(("wide", "narrow"), None),
        P("wide"),
        P(None, "wide"),
        P(),
        P(),
        P(),
        P("wide", "narrow"),
        P("wide", "narrow"),
        P("wide", "narrow"),
        P("narrow", "wide"),
        P("wide", "narrow"),
        P("wide", "narrow"),
        P("narrow", "wide"),
    )
    out_specs = (
        P(("wide", "narrow"), None),
        P(("wide", "narrow"), None),
        P(),
        P(),
        P(),
        P("wide", "narrow"),
        P("wide", "narrow"),
        P("wide", "narrow"),
        P("narrow", "wide"),
        P("wide", "narrow"),
        P("wide", "narrow"),
        P("narrow", "wide"),
    )
    return jax.shard_map(local, mesh=mesh, in_specs=in_specs, out_specs=out_specs, check_vma=False)
```

profile of v0, /device:TPU:0, one launch (start us, length us, event | category | flops | bytes accessed | tf_op | source)
XLA Modules:
  0.0 1946.1 jit_solution(11280851467745284290)
XLA Ops:
  15.8 53.0 %all-gather.18.cloned.1.call-done = bf16[1024,512]{1,0:T(8,128)(2,1)} async-done(((bf16[64,512]{1,0:T(8,128)(2,1)}), bf16[1024,512]{1,0:T(8,128)(2,1)}) %all-gather.18.cloned.1.call-update) | async-done | bytes 1048592 | tf_op jit(solution)/shard_map/all_gather | solution.py:127
  68.8 11.5 all-gather.12.cloned.1.call-done
  84.6 55.0 %all-gather.16.cloned.1.call-done = bf16[1024,512]{1,0:T(8,128)(2,1)} async-done(((bf16[64,512]{1,0:T(8,128)(2,1)}), bf16[1024,512]{1,0:T(8,128)(2,1)}) %all-gather.16.cloned.1.call-update) | async-done | bytes 1048592 | tf_op jit(solution)/shard_map/all_gather | solution.py:126
  143.1 53.2 %all-gather.14.cloned.1.call-done = bf16[1024,512]{1,0:T(8,128)(2,1)} async-done(((bf16[64,512]{1,0:T(8,128)(2,1)}), bf16[1024,512]{1,0:T(8,128)(2,1)}) %all-gather.14.cloned.1.call-update) | async-done | bytes 1048592 | tf_op jit(solution)/shard_map/all_gather | solution.py:125
  200.9 261.7 %while.33 = (s32[]{:T(128)}, bf16[2,512,8,64]{1,3,2,0:T(8,128)(2,1)}, f32[2,8,512,1]{2,1,3,0:T(8,128)}, s32[1024]{0:T(1024)S(1)}, s32[2]{0:T(128)S(1)}, /*index=...) while((s32[]{:T(128)}, ...), condition=%wide.region_4.5_spmd, body=%wide.region_1.4_spmd.sunk | while | flops 2154040320 | bytes 268903200 | solution.py:170
  249.3 10.0 fusion.580
  259.3 9.6 fusion.579
  377.8 10.0 fusion.580
  387.8 9.4 fusion.579
  484.5 63.8 %all-gather.26.cloned.1.call-done = bf16[1024,1408]{1,0:T(8,128)(2,1)} async-done(((bf16[64,1408]{1,0:T(8,128)(2,1)}), bf16[1024,1408]{1,0:T(8,128)(2,1)}) %all-gather.26.cloned.1.call-update) | async-done | bytes 2883600 | tf_op jit(solution)/shard_map/all_gather | solution.py:130
  548.3 11.9 all-gather.22.cloned.1.call-done
  568.7 61.7 %all-gather.24.cloned.1.call-done = bf16[1024,1408]{1,0:T(8,128)(2,1)} async-done(((bf16[64,1408]{1,0:T(8,128)(2,1)}), bf16[1024,1408]{1,0:T(8,128)(2,1)}) %all-gather.24.cloned.1.call-update) | async-done | bytes 2883600 | tf_op jit(solution)/shard_map/all_gather | solution.py:129
  641.5 70.2 %all-gather.28.cloned.1.call-done = bf16[1408,1024]{0,1:T(8,128)(2,1)} async-done(((bf16[1408,64]{0,1:T(8,128)(2,1)}), bf16[1408,1024]{0,1:T(8,128)(2,1)}) %all-gather.28.cloned.1.call-update) | async-done | bytes 2883600 | tf_op jit(solution)/shard_map/all_gather | solution.py:131
  711.8 13.1 multiply_convert_fusion.1
  748.2 11.8 all-gather.32.cloned.1.call-done
  767.6 425.1 %while.34 = (s32[]{:T(128)}, f32[1024,8,64]{0,2,1:T(8,128)}, f32[1024,8,64]{0,2,1:T(8,128)}, f32[96,8]{0,1:T(8,128)}, bf16[2,512,8,64]{1,3,2,0:T(8,128)(2,1)}, /...) while((s32[]{:T(128)}, f32[1024,8,64]{0,2,1:T(8,128)}, ...), condition=%wide.region_12.13_spmd.clone, body=%wide.region_10.12_spmd.clone.sunk | while | flops 4676918272 | bytes 713860288 | solution.py:273
  816.1 9.2 fusion.605
  885.5 18.8 multiply_reduce_fusion.3
  904.3 11.3 multiply_convert_fusion.5
  956.7 9.1 fusion.610
  1024.1 9.2 fusion.605
  1093.7 18.8 multiply_reduce_fusion.3
  1112.5 11.3 multiply_convert_fusion.5
  1123.8 9.4 bitcast_add_fusion.5
  1165.5 9.1 fusion.610
  1257.8 42.1 %all-reduce = (f32[1024]{0:T(1024)}, f32[1024]{0:T(1024)}, f32[96,16]{0,1:T(8,128)}) all-reduce(f32[1024]{0:T(1024)S(1)} %get-tuple-element.407, f32[1024]{0:T(1024)S(1)} %copy-done.65, f32[96,16]{0,1:T(8,128)S(1)} %constant_dynamic-update-slice_fusion), channel_id=1, replica_groups=mesh['wide'=16,'narrow'=2] {'wide','narrow'}, use_global_device_ids=true, to_apply=%region_16.17 | all-reduce | flops 3584 | bytes 28672 | tf_op jit(solution)/shard_map/psum | solution.py:301
  1311.5 80.4 %reduce-scatter.24.cloned.1.call-done = f32[64,512]{1,0:T(8,128)} async-done(((f32[1024,512]{1,0:T(8,128)}), f32[64,512]{1,0:T(8,128)}) %reduce-scatter.24.cloned.1.call-update) | async-done | bytes 131088 | tf_op jit(solution)/shard_map/reduce_scatter | solution.py:307
  1391.9 80.7 %reduce-scatter.20.cloned.1.call-done = f32[64,512]{1,0:T(8,128)} async-done(((f32[1024,512]{1,0:T(8,128)}), f32[64,512]{1,0:T(8,128)}) %reduce-scatter.20.cloned.1.call-update) | async-done | bytes 131088 | tf_op jit(solution)/shard_map/reduce_scatter | solution.py:305
  1472.7 80.8 %reduce-scatter.22.cloned.1.call-done = f32[64,512]{1,0:T(8,128)} async-done(((f32[1024,512]{1,0:T(8,128)}), f32[64,512]{1,0:T(8,128)}) %reduce-scatter.22.cloned.1.call-update) | async-done | bytes 131088 | tf_op jit(solution)/shard_map/reduce_scatter | solution.py:306
  1553.5 125.8 %reduce-scatter.30.cloned.1.call-done = f32[64,1408]{1,0:T(8,128)} async-done(((f32[1024,1408]{1,0:T(8,128)}), f32[64,1408]{1,0:T(8,128)}) %reduce-scatter.30.cloned.1.call-update) | async-done | bytes 360464 | tf_op jit(solution)/shard_map/reduce_scatter | solution.py:310
  1679.3 129.9 %reduce-scatter.28.cloned.1.call-done = f32[64,1408]{1,0:T(8,128)} async-done(((f32[1024,1408]{1,0:T(8,128)}), f32[64,1408]{1,0:T(8,128)}) %reduce-scatter.28.cloned.1.call-update) | async-done | bytes 360464 | tf_op jit(solution)/shard_map/reduce_scatter | solution.py:309
  1809.2 129.9 %reduce-scatter.32.cloned.1.call-done = f32[1408,64]{0,1:T(8,128)} async-done(((f32[1408,1024]{0,1:T(8,128)}), f32[1408,64]{0,1:T(8,128)}) %reduce-scatter.32.cloned.1.call-update) | async-done | bytes 360464 | tf_op jit(solution)/shard_map/reduce_scatter | solution.py:311
  (501 shorter events, 681.8 us)
Async XLA Ops:
  7.2 61.6 %all-gather.18.cloned.1.call-start = ((), (), s32[]{:S(2)}) async-start(), calls=%async_computation.14 | async-start | bytes 1114112 | tf_op jit(solution)/shard_map/all_gather | solution.py:127
  7.9 72.4 %all-gather.12.cloned.1.call-start = ((), (), s32[]{:S(2)}) async-start(), calls=%async_computation.11 | async-start | bytes 3145728 | tf_op jit(solution)/shard_map/all_gather | solution.py:137
  13.8 125.8 %all-gather.16.cloned.1.call-start = ((), (), s32[]{:S(2)}) async-start(), calls=%async_computation.13 | async-start | bytes 1114112 | tf_op jit(solution)/shard_map/all_gather | solution.py:126
  14.6 181.7 %all-gather.14.cloned.1.call-start = ((), (), s32[]{:S(2)}) async-start(), calls=%async_computation.12 | async-start | bytes 1114112 | tf_op jit(solution)/shard_map/all_gather | solution.py:125
  15.1 450.1 %all-gather.20.cloned.1.call-start = ((), (), s32[]{:S(2)}) async-start(), calls=%async_computation.15 | async-start | bytes 1114112 | tf_op jit(solution)/shard_map/all_gather | solution.py:128
  15.7 462.4 %reduce-scatter.12.cloned.1.call-start = ((), (), s32[]{:S(2)}) async-start(), calls=%async_computation.16 | async-start | bytes 3145728 | tf_op jit(solution)/shard_map/reduce_scatter | solution.py:172
  80.3 59.2 %copy-start.72 = (bf16[1024,1024]{1,0:T(8,128)(2,1)S(1)}, bf16[1024,1024]{1,0:T(8,128)(2,1)}, u32[]{:S(2)}) copy-start(bf16[1024,1024]{1,0:T(8,128)(2,1)} %all-gather.12.cloned.1.call-done) | copy-start | bytes 6291460
  143.1 57.8 %copy-start.40 = (s32[2,1024]{1,0:T(2,128)S(1)}, s32[2,1024]{1,0:T(2,128)}, u32[]{:S(2)}) copy-start(s32[2,1024]{1,0:T(2,128)} %param.21) | copy-start | bytes 24580
  143.1 57.8 %copy-start.48 = (s32[1024]{0:T(1024)S(1)}, s32[1024]{0:T(1024)}, u32[]{:S(2)}) copy-start(s32[1024]{0:T(1024)} %param.20) | copy-start | bytes 12292
  469.5 78.8 %all-gather.26.cloned.1.call-start = ((), (), s32[]{:S(2)}) async-start(), calls=%async_computation.19 | async-start | bytes 3063808 | tf_op jit(solution)/shard_map/all_gather | solution.py:130
  470.3 89.9 %all-gather.22.cloned.1.call-start = ((), (), s32[]{:S(2)}) async-start(), calls=%async_computation.17 | async-start | bytes 3145728 | tf_op jit(solution)/shard_map/all_gather | solution.py:182
  470.3 274.7 %copy-start.53 = (f32[1024]{0:T(1024)}, f32[1024]{0:T(1024)S(1)}, u32[]{:S(2)}) copy-start(f32[1024]{0:T(1024)S(1)} %convert_element_type.3947) | copy-start | bytes 12292
  479.7 265.3 %copy-start.57 = (f32[512]{0:T(512)}, f32[512]{0:T(512)S(1)}, u32[]{:S(2)}) copy-start(f32[512]{0:T(512)S(1)} %fusion.462) | copy-start | bytes 6148
  482.4 148.0 %all-gather.24.cloned.1.call-start = ((), (), s32[]{:S(2)}) async-start(), calls=%async_computation.18 | async-start | bytes 3063808 | tf_op jit(solution)/shard_map/all_gather | solution.py:129
  483.2 158.4 %all-gather.30.cloned.1.call-start = ((), (), s32[]{:S(2)}) async-start(), calls=%async_computation.22 | async-start | bytes 3145728 | tf_op jit(solution)/shard_map/all_gather | solution.py:211
  483.7 228.0 %all-gather.28.cloned.1.call-start = ((), (), s32[]{:S(2)}) async-start(), calls=%async_computation.20 | async-start | bytes 3063808 | tf_op jit(solution)/shard_map/all_gather | solution.py:131
  484.5 257.8 %reduce-scatter.16.cloned.1.call-start = ((), (), s32[]{:S(2)}) async-start(), calls=%async_computation.23 | async-start | bytes 3145728 | tf_op jit(solution)/shard_map/reduce_scatter | solution.py:222
  560.2 70.2 %copy-start.73 = (bf16[1024,1024]{1,0:T(8,128)(2,1)S(1)}, bf16[1024,1024]{1,0:T(8,128)(2,1)}, u32[]{:S(2)}) copy-start(bf16[1024,1024]{1,0:T(8,128)(2,1)} %all-gather.22.cloned.1.call-done) | copy-start | bytes 6291460
  733.4 26.6 %all-gather.32.cloned.1.call-start = ((), (), s32[]{:S(2)}) async-start(), calls=%async_computation.24 | async-start | bytes 3145728 | tf_op jit(solution)/shard_map/all_gather | solution.py:233
  748.1 506.9 %reduce-scatter.18.cloned.1.call-start = ((), (), s32[]{:S(2)}) async-start(), calls=%async_computation.25 | async-start | bytes 3145728 | tf_op jit(solution)/shard_map/reduce_scatter | solution.py:289
  1202.9 97.0 %reduce-scatter.14.cloned.1.call-start = ((), (), s32[]{:S(2)}) async-start(), calls=%async_computation.21 | async-start | bytes 3145728 | tf_op jit(solution)/shard_map/reduce_scatter | solution.py:190
  1210.6 100.9 %reduce-scatter.26.cloned.1.call-start = ((), (), s32[]{:S(2)}) async-start(), calls=%async_computation.29 | async-start | bytes 2228224 | tf_op jit(solution)/shard_map/reduce_scatter | solution.py:308
  1214.9 177.0 %reduce-scatter.24.cloned.1.call-start = ((), (), s32[]{:S(2)}) async-start(), calls=%async_computation.28 | async-start | bytes 2228224 | tf_op jit(solution)/shard_map/reduce_scatter | solution.py:307
  1219.4 253.3 %reduce-scatter.20.cloned.1.call-start = ((), (), s32[]{:S(2)}) async-start(), calls=%async_computation.26 | async-start | bytes 2228224 | tf_op jit(solution)/shard_map/reduce_scatter | solution.py:305
  1223.7 329.7 %reduce-scatter.22.cloned.1.call-start = ((), (), s32[]{:S(2)}) async-start(), calls=%async_computation.27 | async-start | bytes 2228224 | tf_op jit(solution)/shard_map/reduce_scatter | solution.py:306
  1228.3 450.9 %reduce-scatter.30.cloned.1.call-start = ((), (), s32[]{:S(2)}) async-start(), calls=%async_computation.31 | async-start | bytes 6127616 | tf_op jit(solution)/shard_map/reduce_scatter | solution.py:310
  1236.8 572.3 %reduce-scatter.28.cloned.1.call-start = ((), (), s32[]{:S(2)}) async-start(), calls=%async_computation.30 | async-start | bytes 6127616 | tf_op jit(solution)/shard_map/reduce_scatter | solution.py:309
  1245.6 693.5 %reduce-scatter.32.cloned.1.call-start = ((), (), s32[]{:S(2)}) async-start(), calls=%async_computation.32 | async-start | bytes 6127616 | tf_op jit(solution)/shard_map/reduce_scatter | solution.py:311
  1254.4 45.6 %copy-start.34 = (bf16[512,1024]{1,0:T(8,128)(2,1)S(1)}, bf16[512,1024]{1,0:T(8,128)(2,1)}, u32[]{:S(2)}) copy-start(bf16[512,1024]{1,0:T(8,128)(2,1)} %reduce-scatter.12.cloned.1.call-done) | copy-start | bytes 3145732
  1254.4 45.6 %copy-start.37 = (bf16[512,1024]{1,0:T(8,128)(2,1)S(1)}, bf16[512,1024]{1,0:T(8,128)(2,1)}, u32[]{:S(2)}) copy-start(bf16[512,1024]{1,0:T(8,128)(2,1)} %param.19) | copy-start | bytes 3145732
  1254.4 45.6 %copy-start.54 = (f32[1024]{0:T(1024)S(1)}, f32[1024]{0:T(1024)}, u32[]{:S(2)}) copy-start(f32[1024]{0:T(1024)} %copy-done.53) | copy-start | bytes 12292
  1299.9 639.1 %copy-start.1 = (bf16[96,16]{0,1:T(8,128)(2,1)S(1)}, bf16[96,16]{0,1:T(8,128)(2,1)}, u32[]{:S(2)}) copy-start(bf16[96,16]{0,1:T(8,128)(2,1)} %param.24) | copy-start | bytes 9220
  (113 other events, 1015.7 us)
Sparse Core Ops, SparseCore 0:
  10.8 57.9 all-gather.17
  70.9 9.3 all-gather.11
  83.1 56.4 all-gather.15
  142.2 54.0 all-gather.13
  198.9 54.0 all-gather.19
  469.6 8.3 reduce-scatter.11
  481.2 67.0 all-gather.25
  550.5 9.6 all-gather.21
  563.3 67.0 all-gather.23
  631.9 9.6 all-gather.29
  644.7 67.0 all-gather.27
  733.6 8.6 reduce-scatter.15
  748.2 11.7 all-gather.31
  1203.0 10.7 reduce-scatter.17
  1216.0 10.8 reduce-scatter.13
  1229.6 81.8 reduce-scatter.25
  1314.2 77.7 reduce-scatter.23
  1394.7 77.9 reduce-scatter.19
  1475.5 77.9 reduce-scatter.21
  1556.2 123.0 reduce-scatter.29
  1682.2 126.9 reduce-scatter.27
  1812.0 126.9 reduce-scatter.31
where the time goes:
time: 1950 us
  waiting for transfers between devices  1050 us (54%)
  matrix products  433 us (22%)
  other arithmetic  253 us (13%)
  local copies, waits for them, and re-layouts  121 us (6%)
  blocking collectives  42.1 us (2%)
  loops' own time  28.9 us (1%)
    dot_general x16, matrix products, block_bias(): jnp.einsum('ai,anf->inf', head_table_entries, indicator_rows, preferred_e...  139 us
    reduce_scatter x1, waiting for transfers between devices, local(): lax.psum_scatter(grad_w_down, 'wide', scatter_dimension=1, tiled=True)  130 us
    reduce_scatter x1, waiting for transfers between devices, local(): lax.psum_scatter(grad_w_gate, 'wide', scatter_dimension=0, tiled=True)  130 us
    reduce_scatter x1, waiting for transfers between devices, local(): lax.psum_scatter(grad_w_up, 'wide', scatter_dimension=0, tiled=True)  126 us
    dot_general x16, local copies, waits for them, and re-layouts, block_bias(): jnp.einsum('ai,anf->inf', head_table_entries, indicator_rows, preferred_e...  81.3 us
    reduce_scatter x1, waiting for transfers between devices, local(): lax.psum_scatter(grad_w_key, 'wide', scatter_dimension=0, tiled=True)  80.8 us
    reduce_scatter x1, waiting for transfers between devices, local(): lax.psum_scatter(grad_w_query, 'wide', scatter_dimension=0, tiled=True)  80.7 us
    reduce_scatter x1, waiting for transfers between devices, local(): lax.psum_scatter(grad_w_value, 'wide', scatter_dimension=0, tiled=True)  80.4 us
  transfers between devices with their start and end apart: 22, of which 19 were waited for; matrix products, arithmetic and copies ran while one was open for 17% of the time, Pallas kernels for 0%

commit v1 on v0

--- a/solution.py
+++ b/solution.py
@@ -10,6 +10,19 @@
 epsilon = 1e-06
 bucket_edges = (1, 2, 3, 4, 5, 6, 7, 8, 12, 16, 23, 32, 46, 64, 91)
 layout_stretch = 4
+
+
+def collect(x, axis, dim):
+    ways = lax.axis_size(axis)
+    up = [(d, (d + 1) % ways) for d in range(ways)]
+    down = [(d, (d - 1) % ways) for d in range(ways)]
+    earlier, later = ([x], [x])
+    for _ in range(ways // 2):
+        earlier.append(lax.ppermute(earlier[-1], axis, up))
+    for _ in range((ways - 1) // 2):
+        later.append(lax.ppermute(later[-1], axis, down))
+    line = jnp.concatenate([*earlier[::-1], *later[1:]], axis=dim)
+    return jnp.roll(line, (lax.axis_index(axis) - ways // 2) * x.shape[dim], axis=dim)
 
 
 def bucket_of(spacing, stretch_factor):
@@ -123,7 +136,7 @@
     head_table_entries = lax.dynamic_slice_in_dim(bias_tables, head_start, heads_local, 1)
     gathered = (
         lax.all_gather(w_query, "wide", axis=0, tiled=True),
-        lax.all_gather(w_key, "wide", axis=0, tiled=True),
+        collect(w_key, "wide", 0),
         lax.all_gather(w_value, "wide", axis=0, tiled=True),
         lax.all_gather(w_out, "wide", axis=1, tiled=True),
         lax.all_gather(w_gate, "wide", axis=0, tiled=True),

time: 1950 us -> 1880 us (0.964)
  waiting for transfers between devices: 1050 us -> 959 us
  starting transfers between devices: 1.1 us -> 45.7 us
    all_gather x1, waiting for transfers between devices: 55 us -> 0.01 us  [local(): lax.all_gather(w_key, 'wide', axis=0, tiled=True)]
    all_gather x1, waiting for transfers between devices: 53.2 us -> 0.02 us  [local(): lax.all_gather(w_query, 'wide', axis=0, tiled=True)]
    ppermute x0 -> x15, starting transfers between devices: none -> 44.6 us  [the longest x7 41.6 us: collect(): later.append(lax.ppermute(later[-1], axis, down))]
    ppermute x0 -> x15, waiting for transfers between devices: none -> 22.9 us  [the longest x8 15.8 us: collect(): earlier.append(lax.ppermute(earlier[-1], axis, up))]
  transfers between devices with their start and end apart: 22 -> 37, of which waited for: 19 -> 30; matrix products, arithmetic and copies ran while one was open for 17% -> 39% of each run, Pallas kernels for 0% -> 0%
where the time goes in v1:
time: 1880 us; the launch traced here: 1870 us
  waiting for transfers between devices  959 us (51%)
  matrix products  432 us (23%)
  other arithmetic  236 us (13%)
  local copies, waits for them, and re-layouts  110 us (6%)
  starting transfers between devices  45.7 us (2%)
  blocking collectives  41.9 us (2%)
  loops' own time  29.4 us (2%)
    reduce_scatter x1, waiting for transfers between devices, local(): lax.psum_scatter(grad_w_gate, 'wide', scatter_dimension=0, tiled=True)  130 us
    reduce_scatter x1, waiting for transfers between devices, local(): lax.psum_scatter(grad_w_down, 'wide', scatter_dimension=1, tiled=True)  130 us
    dot_general x16, matrix products, block_bias(): jnp.einsum('ai,anf->inf', head_table_entries, indicator_rows, preferred_e...  129 us
    reduce_scatter x1, waiting for transfers between devices, local(): lax.psum_scatter(grad_w_up, 'wide', scatter_dimension=0, tiled=True)  126 us
    reduce_scatter x1, waiting for transfers between devices, local(): lax.psum_scatter(grad_w_value, 'wide', scatter_dimension=0, tiled=True)  80.8 us
    reduce_scatter x1, waiting for transfers between devices, local(): lax.psum_scatter(grad_w_query, 'wide', scatter_dimension=0, tiled=True)  80.4 us
    reduce_scatter x1, waiting for transfers between devices, local(): lax.psum_scatter(grad_w_key, 'wide', scatter_dimension=0, tiled=True)  80 us
    dot_general x16, local copies, waits for them, and re-layouts, block_bias(): jnp.einsum('ai,anf->inf', head_table_entries, indicator_rows, preferred_e...  76.3 us
  transfers between devices with their start and end apart: 37, of which 30 were waited for; matrix products, arithmetic and copies ran while one was open for 39% of the time, Pallas kernels for 0%

profile of v1, /device:TPU:0, one launch (start us, length us, event | category | flops | bytes accessed | tf_op | source)
XLA Modules:
  0.0 1868.6 jit_solution(9719851858955649278)
XLA Ops:
  87.0 54.8 %all-gather.16.cloned.1.call-done = bf16[1024,512]{1,0:T(8,128)(2,1)} async-done(((bf16[64,512]{1,0:T(8,128)(2,1)}), bf16[1024,512]{1,0:T(8,128)(2,1)}) %all-gather.16.cloned.1.call-update) | async-done | bytes 1048592 | tf_op jit(solution)/shard_map/all_gather | solution.py:140
  149.5 238.0 %while.33 = (s32[]{:T(128)}, bf16[2,512,8,64]{1,3,2,0:T(8,128)(2,1)}, f32[2,8,512,1]{2,1,3,0:T(8,128)}, s32[1024]{0:T(1024)S(1)}, s32[2]{0:T(128)S(1)}, /*index=...) while((s32[]{:T(128)}, ...), condition=%wide.region_4.5_spmd, body=%wide.region_1.4_spmd.sunk | while | flops 2154040320 | bytes 287777664 | solution.py:183
  247.4 9.2 fusion.584
  364.0 9.0 fusion.584
  409.4 63.6 %all-gather.22.cloned.1.call-done = bf16[1024,1408]{1,0:T(8,128)(2,1)} async-done(((bf16[64,1408]{1,0:T(8,128)(2,1)}), bf16[1024,1408]{1,0:T(8,128)(2,1)}) %all-gather.22.cloned.1.call-update) | async-done | bytes 2883600 | tf_op jit(solution)/shard_map/all_gather | solution.py:142
  473.1 11.9 all-gather.20.cloned.1.call-done
  493.4 61.8 %all-gather.24.cloned.1.call-done = bf16[1024,1408]{1,0:T(8,128)(2,1)} async-done(((bf16[64,1408]{1,0:T(8,128)(2,1)}), bf16[1024,1408]{1,0:T(8,128)(2,1)}) %all-gather.24.cloned.1.call-update) | async-done | bytes 2883600 | tf_op jit(solution)/shard_map/all_gather | solution.py:143
  566.4 70.1 %all-gather.26.cloned.1.call-done = bf16[1408,1024]{0,1:T(8,128)(2,1)} async-done(((bf16[1408,64]{0,1:T(8,128)(2,1)}), bf16[1408,1024]{0,1:T(8,128)(2,1)}) %all-gather.26.cloned.1.call-update) | async-done | bytes 2883600 | tf_op jit(solution)/shard_map/all_gather | solution.py:144
  636.5 13.2 multiply_convert_fusion.1
  673.7 11.1 all-gather.30.cloned.1.call-done
  692.4 420.9 %while.34 = (s32[]{:T(128)}, f32[1024,8,64]{0,2,1:T(8,128)}, f32[1024,8,64]{0,2,1:T(8,128)}, f32[96,8]{0,1:T(8,128)}, bf16[2,512,8,64]{1,3,2,0:T(8,128)(2,1)}, /...) while((s32[]{:T(128)}, f32[1024,8,64]{0,2,1:T(8,128)}, ...), condition=%wide.region_12.13_spmd.clone, body=%wide.region_10.12_spmd.clone.sunk | while | flops 4676918272 | bytes 772548800 | solution.py:286
  762.6 9.2 fusion.608
  798.5 9.5 fusion.604
  808.0 17.3 multiply_reduce_fusion.3
  825.3 11.3 multiply_convert_fusion.5
  842.8 8.8 fusion.613
  851.7 9.4 fusion.612
  870.0 10.7 fusion.614
  968.5 9.2 fusion.608
  1004.4 9.5 fusion.604
  1013.9 17.3 multiply_reduce_fusion.3
  1031.2 11.3 multiply_convert_fusion.5
  1057.6 9.4 fusion.612
  1076.0 10.7 fusion.614
  1178.4 41.9 %all-reduce = (f32[1024]{0:T(1024)}, f32[1024]{0:T(1024)}, f32[96,16]{0,1:T(8,128)}) all-reduce(f32[1024]{0:T(1024)S(1)} %get-tuple-element.407, f32[1024]{0:T(1024)S(1)} %copy-done.68, f32[96,16]{0,1:T(8,128)S(1)} %constant_dynamic-update-slice_fusion.32), channel_id=1, replica_groups=mesh['wide'=16,'narrow'=2] {'wide','narrow'}, use_global_device_ids=true, to_apply=%region_16.17 | all-reduce | flops 3584 | bytes 28672 | tf_op jit(solution)/shard_map/psum | solution.py:314
  1224.6 10.1 reduce-scatter.26.cloned.1.call-done
  1234.7 80.4 %reduce-scatter.20.cloned.1.call-done = f32[64,512]{1,0:T(8,128)} async-done(((f32[1024,512]{1,0:T(8,128)}), f32[64,512]{1,0:T(8,128)}) %reduce-scatter.20.cloned.1.call-update) | async-done | bytes 131088 | tf_op jit(solution)/shard_map/reduce_scatter | solution.py:318
  1315.1 80.0 %reduce-scatter.22.cloned.1.call-done = f32[64,512]{1,0:T(8,128)} async-done(((f32[1024,512]{1,0:T(8,128)}), f32[64,512]{1,0:T(8,128)}) %reduce-scatter.22.cloned.1.call-update) | async-done | bytes 131088 | tf_op jit(solution)/shard_map/reduce_scatter | solution.py:319
  1395.1 80.8 %reduce-scatter.24.cloned.1.call-done = f32[64,512]{1,0:T(8,128)} async-done(((f32[1024,512]{1,0:T(8,128)}), f32[64,512]{1,0:T(8,128)}) %reduce-scatter.24.cloned.1.call-update) | async-done | bytes 131088 | tf_op jit(solution)/shard_map/reduce_scatter | solution.py:320
  1475.9 126.0 %reduce-scatter.30.cloned.1.call-done = f32[64,1408]{1,0:T(8,128)} async-done(((f32[1024,1408]{1,0:T(8,128)}), f32[64,1408]{1,0:T(8,128)}) %reduce-scatter.30.cloned.1.call-update) | async-done | bytes 360464 | tf_op jit(solution)/shard_map/reduce_scatter | solution.py:323
  1601.8 129.9 %reduce-scatter.28.cloned.1.call-done = f32[64,1408]{1,0:T(8,128)} async-done(((f32[1024,1408]{1,0:T(8,128)}), f32[64,1408]{1,0:T(8,128)}) %reduce-scatter.28.cloned.1.call-update) | async-done | bytes 360464 | tf_op jit(solution)/shard_map/reduce_scatter | solution.py:322
  1731.7 129.9 %reduce-scatter.32.cloned.1.call-done = f32[1408,64]{0,1:T(8,128)} async-done(((f32[1408,1024]{0,1:T(8,128)}), f32[1408,64]{0,1:T(8,128)}) %reduce-scatter.32.cloned.1.call-update) | async-done | bytes 360464 | tf_op jit(solution)/shard_map/reduce_scatter | solution.py:324
  (589 shorter events, 696.6 us)
Async XLA Ops:
  7.2 75.6 %all-gather.14.cloned.1.call-start = ((), (), s32[]{:S(2)}) async-start(), calls=%async_computation.12 | async-start | bytes 1114112 | tf_op jit(solution)/shard_map/all_gather | solution.py:138
  7.9 74.9 %all-gather.12.cloned.1.call-start = ((), (), s32[]{:S(2)}) async-start(), calls=%async_computation.11 | async-start | bytes 3145728 | tf_op jit(solution)/shard_map/all_gather | solution.py:150
  13.9 128.0 %all-gather.16.cloned.1.call-start = ((), (), s32[]{:S(2)}) async-start(), calls=%async_computation.13 | async-start | bytes 1114112 | tf_op jit(solution)/shard_map/all_gather | solution.py:140
  14.6 375.5 %all-gather.18.cloned.1.call-start = ((), (), s32[]{:S(2)}) async-start(), calls=%async_computation.14 | async-start | bytes 1114112 | tf_op jit(solution)/shard_map/all_gather | solution.py:141
  14.7 9.2 collective-permute-start
  23.9 8.1 collective-permute-start.1
  23.9 8.1 collective-permute-start.8
  32.0 8.1 collective-permute-start.9
  39.9 8.4 collective-permute-start.3
  40.1 8.2 collective-permute-start.10
  48.3 9.9 collective-permute-start.11
  56.1 8.9 collective-permute-start.5
  58.2 8.5 collective-permute-start.12
  65.0 337.9 %reduce-scatter.12.cloned.1.call-start = ((), (), s32[]{:S(2)}) async-start(), calls=%async_computation.15 | async-start | bytes 3145728 | tf_op jit(solution)/shard_map/reduce_scatter | solution.py:185
  66.7 8.0 collective-permute-start.13
  394.4 78.7 %all-gather.22.cloned.1.call-start = ((), (), s32[]{:S(2)}) async-start(), calls=%async_computation.17 | async-start | bytes 3063808 | tf_op jit(solution)/shard_map/all_gather | solution.py:142
  395.0 89.9 %all-gather.20.cloned.1.call-start = ((), (), s32[]{:S(2)}) async-start(), calls=%async_computation.16 | async-start | bytes 3145728 | tf_op jit(solution)/shard_map/all_gather | solution.py:195
  407.3 147.8 %all-gather.24.cloned.1.call-start = ((), (), s32[]{:S(2)}) async-start(), calls=%async_computation.18 | async-start | bytes 3063808 | tf_op jit(solution)/shard_map/all_gather | solution.py:143
  408.1 158.4 %all-gather.28.cloned.1.call-start = ((), (), s32[]{:S(2)}) async-start(), calls=%async_computation.21 | async-start | bytes 3145728 | tf_op jit(solution)/shard_map/all_gather | solution.py:224
  408.8 227.7 %all-gather.26.cloned.1.call-start = ((), (), s32[]{:S(2)}) async-start(), calls=%async_computation.19 | async-start | bytes 3063808 | tf_op jit(solution)/shard_map/all_gather | solution.py:144
  409.4 257.7 %reduce-scatter.16.cloned.1.call-start = ((), (), s32[]{:S(2)}) async-start(), calls=%async_computation.22 | async-start | bytes 3145728 | tf_op jit(solution)/shard_map/reduce_scatter | solution.py:235
  658.2 26.6 %all-gather.30.cloned.1.call-start = ((), (), s32[]{:S(2)}) async-start(), calls=%async_computation.23 | async-start | bytes 3145728 | tf_op jit(solution)/shard_map/all_gather | solution.py:246
  672.9 447.5 %all-gather.32.cloned.1.call-start = ((), (), s32[]{:S(2)}) async-start(), calls=%async_computation.24 | async-start | bytes 1114112 | tf_op jit(solution)/shard_map/all_gather | solution.py:216
  673.7 502.0 %reduce-scatter.18.cloned.1.call-start = ((), (), s32[]{:S(2)}) async-start(), calls=%async_computation.25 | async-start | bytes 3145728 | tf_op jit(solution)/shard_map/reduce_scatter | solution.py:302
  1125.9 94.4 %reduce-scatter.14.cloned.1.call-start = ((), (), s32[]{:S(2)}) async-start(), calls=%async_computation.20 | async-start | bytes 3145728 | tf_op jit(solution)/shard_map/reduce_scatter | solution.py:203
  1133.5 101.2 %reduce-scatter.26.cloned.1.call-start = ((), (), s32[]{:S(2)}) async-start(), calls=%async_computation.29 | async-start | bytes 2228224 | tf_op jit(solution)/shard_map/reduce_scatter | solution.py:321
  1137.9 177.2 %reduce-scatter.20.cloned.1.call-start = ((), (), s32[]{:S(2)}) async-start(), calls=%async_computation.26 | async-start | bytes 2228224 | tf_op jit(solution)/shard_map/reduce_scatter | solution.py:318
  1142.4 252.7 %reduce-scatter.22.cloned.1.call-start = ((), (), s32[]{:S(2)}) async-start(), calls=%async_computation.27 | async-start | bytes 2228224 | tf_op jit(solution)/shard_map/reduce_scatter | solution.py:319
  1146.8 329.0 %reduce-scatter.24.cloned.1.call-start = ((), (), s32[]{:S(2)}) async-start(), calls=%async_computation.28 | async-start | bytes 2228224 | tf_op jit(solution)/shard_map/reduce_scatter | solution.py:320
  1151.6 450.2 %reduce-scatter.30.cloned.1.call-start = ((), (), s32[]{:S(2)}) async-start(), calls=%async_computation.31 | async-start | bytes 6127616 | tf_op jit(solution)/shard_map/reduce_scatter | solution.py:323
  1158.8 572.9 %reduce-scatter.28.cloned.1.call-start = ((), (), s32[]{:S(2)}) async-start(), calls=%async_computation.30 | async-start | bytes 6127616 | tf_op jit(solution)/shard_map/reduce_scatter | solution.py:322
  1166.2 695.4 %reduce-scatter.32.cloned.1.call-start = ((), (), s32[]{:S(2)}) async-start(), calls=%async_computation.32 | async-start | bytes 6127616 | tf_op jit(solution)/shard_map/reduce_scatter | solution.py:324
  (140 other events, 2573.7 us)
Sparse Core Ops, SparseCore 0:
  10.8 61.1 all-gather.13
  74.1 8.3 all-gather.11
  85.3 56.4 all-gather.15
  144.4 54.0 all-gather.17
  394.5 8.3 reduce-scatter.11
  406.0 67.0 all-gather.21
  475.3 9.6 all-gather.19
  488.1 67.0 all-gather.23
  556.8 9.6 all-gather.27
  569.4 67.0 all-gather.25
  658.4 8.6 reduce-scatter.15
  673.0 11.7 all-gather.29
  687.6 56.4 all-gather.31
  1126.0 10.7 reduce-scatter.17
  1139.0 10.8 reduce-scatter.13
  1152.5 82.1 reduce-scatter.25
  1237.4 77.6 reduce-scatter.19
  1317.8 77.2 reduce-scatter.21
  1397.9 77.8 reduce-scatter.23
  1478.6 123.1 reduce-scatter.29
  1604.7 126.9 reduce-scatter.27
  1734.6 126.9 reduce-scatter.31
